TPU v7x, 32 devices: a whole 2x2x4 slice. The times are simulated.
32 devices in a mesh: req: 8 (over y, x, core), mdl: 4 (over z).
Axes of the slice: x: 2, y: 2, z: 4, core: 2. Of those that a mesh axis runs over, the one named last changes fastest.
Arguments:
- tokens: bfloat16 [256, 4, 2048], P('req', None, 'mdl'), may hold values from -6 to 6
- counts: int32 [256], P('req'), may hold values from 1 to 4
- new_owner: int32 [256], replicated, may hold values from 0 to 255, as said below
- wkv_state: float32 [256, 32, 4096], P('req', 'mdl'), may hold values from -12 to 12
- att_shift: bfloat16 [256, 2048], P('req', 'mdl'), may hold values from -6 to 6
- ffn_shift: bfloat16 [256, 2048], P('req', 'mdl'), may hold values from -6 to 6
- norm_params: float32 [4, 2048], replicated, may hold values from 0.25 to 1.75
- mix_coeffs: float32 [7, 2048], replicated, may hold values from 0 to 1
- head_params: float32 [7, 2048], P(None, 'mdl'), may hold values from -6 to 2
- recept_weight: bfloat16 [2048, 2048], P(None, 'mdl'), may hold values from -0.125 to 0.125
- key_weight: bfloat16 [2048, 2048], P(None, 'mdl'), may hold values from -0.125 to 0.125
- value_weight: bfloat16 [2048, 2048], P(None, 'mdl'), may hold values from -0.125 to 0.125
- output_weight: bfloat16 [2048, 2048], P('mdl'), may hold values from -0.125 to 0.125
- decay_down: bfloat16 [2048, 96], P('mdl'), may hold values from -0.125 to 0.125
- decay_up: bfloat16 [96, 2048], P(None, 'mdl'), may hold values from -0.625 to 0.625
- alpha_down: bfloat16 [2048, 96], P('mdl'), may hold values from -0.125 to 0.125
- alpha_up: bfloat16 [96, 2048], P(None, 'mdl'), may hold values from -0.625 to 0.625
- gate_down: bfloat16 [2048, 256], P('mdl'), may hold values from -0.125 to 0.125
- gate_up: bfloat16 [256, 2048], P(None, 'mdl'), may hold values from -0.375 to 0.375
- ffn_key_weight: bfloat16 [2048, 4096], P(None, 'mdl'), may hold values from -0.125 to 0.125
- ffn_value_weight: bfloat16 [4096, 2048], P('mdl'), may hold values from -0.09375 to 0.09375
Outputs:
- block_output: bfloat16 [256, 4, 2048], P('req', None, 'mdl')
- new_state: float32 [256, 32, 4096], P('req', 'mdl')
- new_att_shift: bfloat16 [256, 2048], P('req', 'mdl')
- new_ffn_shift: bfloat16 [256, 2048], P('req', 'mdl')
Inputs may be any that keep to these rules, and one draw needn't show every extreme that they name: new_owner is a permutation: the states of request i move to position new_owner[i]. Of the 32 requests of each aligned block of positions, exactly 4 move into each aligned block.
All inputs are finite; a program needn't handle non-finite values.
Results may differ from a plain program's by a relative error of at most 0.0095.
Values may be sent and summed in bfloat16 or wider, within the bound.
No kernel may reach another device: no remote copies, remote signals or barrier semaphores. Data moves between devices by JAX's collectives and lax.ppermute only.
A program may use at most 256 MiB of HBM per device.

v0:
```python
import jax
import jax.numpy as jnp
from jax import lax
from jax.sharding import PartitionSpec as P


def layer_norm(stream, gain_row, offset):
    center = stream - jnp.mean(stream, axis=-1, keepdims=True)
    spread = jnp.mean(center * center, axis=-1, keepdims=True)
    return center / jnp.sqrt(spread + 1e-05) * gain_row + offset


def project(inputs, weight):
    return jnp.dot(inputs, weight, preferred_element_type=jnp.float32)


def split_heads(source, head_size):
    sequence_batch_count, decode_loop_steps_count, feature_count = source.shape
    return source.reshape(
        sequence_batch_count, decode_loop_steps_count, feature_count // head_size, head_size
    )


def advance(wkv_square, decay_now, key_now, value_now, unit_now, alpha_now, recept_now, is_valid):
    removal = -jnp.sum(wkv_square * unit_now[:, :, None, :], axis=-1)
    updated = (
        wkv_square * decay_now[:, :, None, :]
        + removal[..., None] * (unit_now * alpha_now)[:, :, None, :]
        + value_now[..., None] * key_now[:, :, None, :]
    )
    memory_matrix_product = jnp.sum(updated * recept_now[:, :, None, :], axis=-1)
    return (jnp.where(is_valid[:, None, None, None], updated, wkv_square), memory_matrix_product)


def prepare_keys(key_proj, in_context, learned_weights, head_size):
    scaled = split_heads(key_proj * learned_weights[2], head_size)
    key_unit = scaled / jnp.sqrt(jnp.sum(scaled * scaled, axis=-1, keepdims=True) + 1e-06)
    lookup_adjust_factor = key_proj * (1.0 + (in_context - 1.0) * learned_weights[3])
    return (key_unit.reshape(key_proj.shape), lookup_adjust_factor)


def run_heads(
    wkv_flat,
    decay_rate,
    lookup_adjust_factor,
    values,
    key_unit,
    in_context,
    acceptance_matrix_lines,
    live_mask,
    head_size,
):
    sequence_batch_count, decode_loop_steps_count, feature_count = acceptance_matrix_lines.shape
    head_count = feature_count // head_size
    decay_heads = split_heads(decay_rate, head_size)
    keymod_heads = split_heads(lookup_adjust_factor, head_size)
    payload_each_group = split_heads(values, head_size)
    unit_heads = split_heads(key_unit, head_size)
    alpha_heads = split_heads(in_context, head_size)
    recept_heads = split_heads(acceptance_matrix_lines, head_size)
    wkv_square = wkv_flat.reshape(sequence_batch_count, head_count, head_size, head_size)
    readouts = []
    for position in range(decode_loop_steps_count):
        wkv_square, memory_matrix_product = advance(
            wkv_square,
            decay_heads[:, position],
            keymod_heads[:, position],
            payload_each_group[:, position],
            unit_heads[:, position],
            alpha_heads[:, position],
            recept_heads[:, position],
            live_mask[:, position] > 0.5,
        )
        readouts.append(memory_matrix_product)
    stacked = jnp.stack(readouts, axis=1).reshape(
        sequence_batch_count, decode_loop_steps_count, feature_count
    )
    return (stacked, wkv_square.reshape(sequence_batch_count, head_count, head_size * head_size))


def finish_heads(
    memory_matrix_product,
    acceptance_matrix_lines,
    lookup_adjust_factor,
    values,
    sigmoid_scaling_entries,
    learned_weights,
    head_size,
):
    stacked = split_heads(memory_matrix_product, head_size)
    center = stacked - jnp.mean(stacked, axis=-1, keepdims=True)
    spread = jnp.mean(center * center, axis=-1, keepdims=True)
    layernormed_activations = (center / jnp.sqrt(spread + 0.00064)).reshape(
        memory_matrix_product.shape
    ) * learned_weights[5] + learned_weights[6]
    extra_term_share = jnp.sum(
        split_heads(acceptance_matrix_lines * lookup_adjust_factor * learned_weights[4], head_size),
        axis=-1,
        keepdims=True,
    ) * split_heads(values, head_size)
    return (
        (layernormed_activations + extra_term_share.reshape(memory_matrix_product.shape))
        * sigmoid_scaling_entries
    ).astype(jnp.bfloat16)


def per_device(
    tokens,
    counts,
    new_owner,
    wkv_state,
    att_shift,
    ffn_shift,
    norm_params,
    mix_coeffs,
    head_params,
    recept_weight,
    key_weight,
    value_weight,
    output_weight,
    decay_down,
    decay_up,
    alpha_down,
    alpha_up,
    gate_down,
    gate_up,
    ffn_key_weight,
    ffn_value_weight,
):
    groups = lax.axis_size("req")
    sequence_batch_count, decode_loop_steps_count, local_width = tokens.shape
    per_pair = sequence_batch_count // groups
    req_rank = lax.axis_index("req")
    column_start = lax.axis_index("mdl") * local_width
    head_size = local_width // wkv_state.shape[1]
    row_count = sequence_batch_count * decode_loop_steps_count
    shape_three = (sequence_batch_count, decode_loop_steps_count, local_width)
    slot_ids = jnp.arange(decode_loop_steps_count, dtype=jnp.int32)
    live_mask = (slot_ids[None, :] < counts[:, None]).astype(jnp.float32)
    own_block = lax.dynamic_slice_in_dim(
        new_owner, req_rank * sequence_batch_count, sequence_batch_count
    )
    sending = jnp.argsort(own_block)
    sorted_rows = jnp.sort(new_owner.reshape(groups, sequence_batch_count), axis=1)
    arriving = (
        lax.dynamic_slice_in_dim(sorted_rows, req_rank * per_pair, per_pair, 1)
        - req_rank * sequence_batch_count
    )
    placing = jnp.argsort(arriving.reshape(-1))
    sent_state = wkv_state[sending].reshape((groups, per_pair) + wkv_state.shape[1:])
    sent_att = att_shift[sending].astype(jnp.float32).reshape(groups, per_pair, local_width)
    sent_ffn = ffn_shift[sending].astype(jnp.float32).reshape(groups, per_pair, local_width)
    got_state, got_att, got_ffn = (
        lax.all_to_all(sent_state, "req", split_axis=0, concat_axis=0, tiled=True),
        lax.all_to_all(sent_att, "req", split_axis=0, concat_axis=0, tiled=True),
        lax.all_to_all(sent_ffn, "req", split_axis=0, concat_axis=0, tiled=True),
    )
    moved_state = got_state.reshape((sequence_batch_count,) + wkv_state.shape[1:])[placing]
    moved_att = got_att.reshape(sequence_batch_count, local_width)[placing].astype(jnp.bfloat16)
    moved_ffn = got_ffn.reshape(sequence_batch_count, local_width)[placing].astype(jnp.bfloat16)
    full_tokens = lax.all_gather(tokens, "mdl", axis=2, tiled=True)
    full_stream = full_tokens.astype(jnp.float32)
    entire_channel_count = full_tokens.shape[2]
    prev_att, prev_ffn = (
        lax.all_gather(moved_att, "mdl", axis=1, tiled=True),
        lax.all_gather(moved_ffn, "mdl", axis=1, tiled=True),
    )
    normed_one = layer_norm(full_stream, norm_params[0], norm_params[1])
    before_one = jnp.concatenate(
        [prev_att.astype(jnp.float32)[:, None], normed_one[:, :-1]], axis=1
    )
    delta_one = before_one - normed_one
    normed_local = lax.dynamic_slice_in_dim(normed_one, column_start, local_width, 2)

    def mixed_input(mix_index):
        return (
            (normed_one + delta_one * mix_coeffs[mix_index])
            .astype(jnp.bfloat16)
            .reshape(row_count, entire_channel_count)
        )

    decay_full, alpha_full, gate_full = (
        lax.all_gather(decay_down, "mdl", axis=0, tiled=True),
        lax.all_gather(alpha_down, "mdl", axis=0, tiled=True),
        lax.all_gather(gate_down, "mdl", axis=0, tiled=True),
    )
    decay_sum = project(mixed_input(1), decay_full)
    alpha_sum = project(mixed_input(4), alpha_full)
    gate_sum = project(mixed_input(5), gate_full)
    decay_low = jnp.tanh(decay_sum).astype(jnp.bfloat16)
    alpha_low = alpha_sum.astype(jnp.bfloat16)
    gate_low = jax.nn.sigmoid(gate_sum).astype(jnp.bfloat16)
    decay_rate = jnp.exp(
        -0.606531 * jax.nn.sigmoid(head_params[0] + project(decay_low, decay_up))
    ).reshape(shape_three)
    in_context = jax.nn.sigmoid(head_params[1] + project(alpha_low, alpha_up)).reshape(shape_three)
    sigmoid_scaling_entries = project(gate_low, gate_up).reshape(shape_three)
    acceptance_matrix_lines = project(mixed_input(0), recept_weight).reshape(shape_three)
    key_proj = project(mixed_input(2), key_weight).reshape(shape_three)
    values = project(mixed_input(3), value_weight).reshape(shape_three)
    key_unit, lookup_adjust_factor = prepare_keys(key_proj, in_context, head_params, head_size)
    memory_matrix_product, new_state = run_heads(
        moved_state,
        decay_rate,
        lookup_adjust_factor,
        values,
        key_unit,
        in_context,
        acceptance_matrix_lines,
        live_mask,
        head_size,
    )
    attention_group_result = finish_heads(
        memory_matrix_product,
        acceptance_matrix_lines,
        lookup_adjust_factor,
        values,
        sigmoid_scaling_entries,
        head_params,
        head_size,
    )
    attended_term = project(attention_group_result.reshape(row_count, local_width), output_weight)
    attended = lax.psum_scatter(attended_term, "mdl", scatter_dimension=1, tiled=True).reshape(
        shape_three
    )
    midstream = (tokens.astype(jnp.float32) + attended).astype(jnp.bfloat16)
    full_mid = lax.all_gather(midstream, "mdl", axis=2, tiled=True)
    normed_two = layer_norm(full_mid.astype(jnp.float32), norm_params[2], norm_params[3])
    before_two = jnp.concatenate(
        [prev_ffn.astype(jnp.float32)[:, None], normed_two[:, :-1]], axis=1
    )
    ffn_in = (
        (normed_two + (before_two - normed_two) * mix_coeffs[6])
        .astype(jnp.bfloat16)
        .reshape(row_count, entire_channel_count)
    )
    hidden = jnp.square(jax.nn.relu(project(ffn_in, ffn_key_weight))).astype(jnp.bfloat16)
    ffn_out = (
        lax.psum_scatter(
            project(hidden, ffn_value_weight).astype(jnp.bfloat16),
            "mdl",
            scatter_dimension=1,
            tiled=True,
        )
        .astype(jnp.float32)
        .reshape(shape_three)
    )
    block_output = jnp.where(
        live_mask[..., None] > 0.5, midstream.astype(jnp.float32) + ffn_out, 0.0
    ).astype(jnp.bfloat16)
    chosen = (slot_ids[None, :] == (counts - 1)[:, None]).astype(jnp.float32)
    normed_two_local = lax.dynamic_slice_in_dim(normed_two, column_start, local_width, 2)
    new_att_shift = jnp.sum(normed_local * chosen[..., None], axis=1).astype(jnp.bfloat16)
    new_ffn_shift = jnp.sum(normed_two_local * chosen[..., None], axis=1).astype(jnp.bfloat16)
    return (block_output, new_state, new_att_shift, new_ffn_shift)


def solution(mesh):
    return jax.shard_map(
        per_device,
        mesh=mesh,
        in_specs=(
            P("req", None, "mdl"),
            P("req"),
            P(),
            P("req", "mdl", None),
            P("req", "mdl"),
            P("req", "mdl"),
            P(),
            P(),
            P(None, "mdl"),
            P(None, "mdl"),
            P(None, "mdl"),
            P(None, "mdl"),
            P("mdl", None),
            P("mdl", None),
            P(None, "mdl"),
            P("mdl", None),
            P(None, "mdl"),
            P("mdl", None),
            P(None, "mdl"),
            P(None, "mdl"),
            P("mdl", None),
        ),
        out_specs=(P("req", None, "mdl"), P("req", "mdl", None), P("req", "mdl"), P("req", "mdl")),
        check_vma=False,
    )
```

profile of v0, /device:TPU:0, one launch (start us, length us, event | category | flops | bytes accessed | tf_op | source)
XLA Modules:
  0.0 439.1 jit_solution(6680961267923316029)
XLA Ops:
  12.3 5.2 %all-to-all-start.1 = ((bf16[8,4,512]{2,1,0:T(4,128)(2,1)}), bf16[8,4,512]{2,1,0:T(4,128)(2,1)S(1)}, u32[]{:S(2)}, u32[]{:S(2)}) async-start(bf16[8,4,512]{2,1,0:T(4,128)(2,1)} %reshape.354), calls=%async_computation.1 | async-start | bytes 65536 | tf_op jit(solution)/shard_map/all_to_all | solution.py:155
  27.7 20.2 %all_gather.23 = bf16[2048,96]{0,1:T(8,128)(2,1)} all-gather(bf16[512,96]{0,1:T(8,128)(2,1)} %param.34), channel_id=1, replica_groups=mesh['req'=8,'mdl'=4] {'mdl'}, dimensions={0}, use_global_device_ids=true | all-gather | bytes 491520 | tf_op jit(solution)/shard_map/all_gather | solution.py:183
  47.9 15.2 %all_gather.24 = bf16[2048,96]{0,1:T(8,128)(2,1)S(1)} all-gather(bf16[512,96]{0,1:T(8,128)(2,1)} %param.36), channel_id=1, replica_groups=mesh['req'=8,'mdl'=4] {'mdl'}, dimensions={0}, use_global_device_ids=true | all-gather | bytes 491520 | tf_op jit(solution)/shard_map/all_gather | solution.py:184
  63.2 14.9 %all_gather.21 = bf16[32,4,2048]{2,1,0:T(4,128)(2,1)S(1)} all-gather(bf16[32,4,512]{2,1,0:T(4,128)(2,1)} %param.21), channel_id=1, replica_groups=mesh['req'=8,'mdl'=4] {'mdl'}, dimensions={2}, use_global_device_ids=true | all-gather | bytes 655360 | tf_op jit(solution)/shard_map/all_gather | solution.py:161
  84.3 5.0 %gather_fusion = f32[32,8,4096]{2,1,0:T(8,128)} fusion(f32[32,8,4096]{2,1,0:T(8,128)} %param.24, s32[1024]{0:T(1024)S(1)} %pad_clamp_fusion.1), kind=kCustom, calls=%fused_computation | custom fusion | bytes 8388736 | tf_op jit(solution)/shard_map/gather | solution.py:150
  89.4 4.8 %all-to-all-start = ((f32[8,4,8,4096]{3,2,1,0:T(8,128)}), f32[8,4,8,4096]{3,2,1,0:T(8,128)}, u32[]{:S(2)}, u32[]{:S(2)}) async-start(f32[8,4,8,4096]{3,2,1,0:T(8,128)} %bitcast.175), calls=%async_computation | async-start | bytes 8388608 | tf_op jit(solution)/shard_map/all_to_all | solution.py:154
  94.9 13.7 %all_gather.22 = bf16[32,2048]{1,0:T(8,128)(2,1)S(1)} all-gather(bf16[32,512]{1,0:T(8,128)(2,1)S(1)} %gather_fusion.3), channel_id=1, replica_groups=mesh['req'=8,'mdl'=4] {'mdl'}, dimensions={1}, use_global_device_ids=true | all-gather | bytes 163840 | tf_op jit(solution)/shard_map/all_gather | solution.py:165
  157.1 5.1 %gather_fusion.1 = f32[32,8,4096]{2,1,0:T(8,128)} fusion(f32[32,8,4096]{2,1,0:T(8,128)} %bitcast.1, s32[1024]{0:T(1024)} %copy-done.21), kind=kCustom, calls=%fused_computation.1 | custom fusion | bytes 8388736 | tf_op jit(solution)/shard_map/gather | solution.py:158
  162.2 8.3 %reshape.338 = f32[32,8,64,64]{3,2,1,0:T(8,128)} reshape(f32[32,8,4096]{2,1,0:T(8,128)} %gather_fusion.1) | data formatting | bytes 8388608 | tf_op jit(solution)/shard_map/reshape | solution.py:61
  170.5 5.8 %multiply_reduce_fusion.7 = f32[32,8,64]{2,1,0:T(8,128)S(1)} fusion(f32[32,8,64,64]{3,2,1,0:T(8,128)} %reshape.338, f32[32,8,64]{2,1,0:T(8,128)S(1)} %get-tuple-element.90), kind=kLoop, calls=%fused_computation.16 | loop fusion | flops 2080768 | bytes 4325376 | tf_op jit(solution)/shard_map/reduce_sum | solution.py:25
  176.4 11.0 %multiply_reduce_fusion.6 = (f32[32,8,64]{2,1,0:T(8,128)S(1)}, f32[32,8,64]{2,1,0:T(8,128)S(1)}) fusion(f32[32,8,64]{2,1,0:T(8,128)S(1)} %copy-done.8, f32[32,8,64,64]{3,2,1,0:T(8,128)S(1)} %copy-done.2, f32[32,8,64]{2,1,0:T(8,128)S(1)} %get-tuple-element.51, f32[32,8,64]{2,1,0:T(8,128)S(1)} %get-tuple-element.30, f32[32,8,64]{2,1,0:T(8,128)S(1)} %neg.38, ...), kind=kLoop, calls=%fused_computation.14 | loop fusion | flops 10452992 | bytes 4784160 | tf_op jit(solution)/shard_map/reduce_sum | solution.py:31
  188.8 18.7 %multiply_reduce_fusion.3 = (f32[32,8,64]{2,1,0:T(8,128)S(1)}, f32[32,8,64,64]{3,2,1,0:T(8,128)}, f32[32,8,64]{2,1,0:T(8,128)S(1)}, f32[32,8,64,64]{3,2,1,0:T(8,...) fusion(f32[32,8,64]{2,1,0:T(8,128)} %get-tuple-element.92, ...), kind=kLoop, calls=%fused_computation.10 | loop fusion | flops 16744448 | bytes 26083392 | tf_op jit(solution)/shard_map/reduce_sum | solution.py:25
  208.3 12.5 %multiply_reduce_fusion.2 = (f32[32,8,64]{2,1,0:T(8,128)S(1)}, f32[32,8,64]{2,1,0:T(8,128)S(1)}, f32[32,8,64,64]{3,2,1,0:T(8,128)}, f32[32,8,64,64]{3,2,1,0:T(8,128)}) fusion(f32[32,8,64]{2,1,0:T(8,128)} %get-tuple-element.34, f32[32,8,64,64]{3,2,1,0:T(8,128)} %get-tuple-element.18, f32[32,8,64]{2,1,0:T(8,128)S(1)} %get-tuple-element.48, ...), kind=kLoop, calls=%fused_computation.8 | loop fusion | flops 10452992 | bytes 13172768 | tf_op jit(solution)/shard_map/reduce_sum | solution.py:31
  222.2 15.5 %broadcast_multiply_fusion.1 = (f32[32,8,64,64]{3,2,1,0:T(8,128)}, f32[32,8,64]{2,1,0:T(8,128)S(1)}, f32[32,8,64,64]{3,2,1,0:T(8,128)}) fusion(f32[32,8,64]{2,1,0:T(8,128)} %get-tuple-element.31, f32[32,8,64]{2,1,0:T(8,128)} %neg.42, f32[32,8,64]{2,1,0:T(8,128)} %get-tuple-element.33, f32[32,8,64]{2,1,0:T(8,128)} %get-tuple-element.40, ...), kind=kLoop, calls=%fused_computation.19 | loop fusion | flops 13615104 | bytes 13369376 | tf_op jit(solution)/shard_map/mul | solution.py:28
  246.2 4.5 %all-to-all-start.2 = ((bf16[8,4,512]{2,1,0:T(4,128)(2,1)}), bf16[8,4,512]{2,1,0:T(4,128)(2,1)S(1)}, u32[]{:S(2)}, u32[]{:S(2)}) async-start(bf16[8,4,512]{2,1,0:T(4,128)(2,1)} %reshape.356), calls=%async_computation.3 | async-start | bytes 65536 | tf_op jit(solution)/shard_map/all_to_all | solution.py:156
  250.9 4.6 %all-to-all-done.2 = bf16[8,4,512]{2,1,0:T(4,128)(2,1)S(1)} async-done(((bf16[8,4,512]{2,1,0:T(4,128)(2,1)}), bf16[8,4,512]{2,1,0:T(4,128)(2,1)S(1)}, u32[]{:S(2)}, u32[]{:S(2)}) %all-to-all-start.2) | async-done | bytes 32800 | tf_op jit(solution)/shard_map/all_to_all | solution.py:156
  256.3 14.6 %all_gather.27 = bf16[32,2048]{1,0:T(8,128)(2,1)S(1)} all-gather(bf16[32,512]{1,0:T(8,128)(2,1)S(1)} %gather_fusion.5), channel_id=1, replica_groups=mesh['req'=8,'mdl'=4] {'mdl'}, dimensions={1}, use_global_device_ids=true | all-gather | bytes 163840 | tf_op jit(solution)/shard_map/all_gather | solution.py:166
  274.9 8.1 %mul.647 = f32[32,8,4096]{2,1,0:T(8,128)} reshape(f32[32,8,64,64]{3,2,1,0:T(8,128)} %mul.597) | data formatting | bytes 8388608 | tf_op jit(solution)/shard_map/mul | solution.py:27
  286.7 7.9 %mul.639 = f32[32,8,4096]{2,1,0:T(8,128)} reshape(f32[32,8,64,64]{3,2,1,0:T(8,128)} %mul.561) | data formatting | bytes 8388608 | tf_op jit(solution)/shard_map/mul | solution.py:27
  298.3 7.9 %mul.643 = f32[32,8,4096]{2,1,0:T(8,128)} reshape(f32[32,8,64,64]{3,2,1,0:T(8,128)} %mul.579) | data formatting | bytes 8388608 | tf_op jit(solution)/shard_map/mul | solution.py:27
  309.9 7.9 %mul.635 = f32[32,8,4096]{2,1,0:T(8,128)} reshape(f32[32,8,64,64]{3,2,1,0:T(8,128)} %mul.523) | data formatting | bytes 8388608 | tf_op jit(solution)/shard_map/mul | solution.py:27
  317.8 7.9 %mul.637 = f32[32,8,4096]{2,1,0:T(8,128)} reshape(f32[32,8,64,64]{3,2,1,0:T(8,128)} %get-tuple-element.52) | data formatting | bytes 8388608 | tf_op jit(solution)/shard_map/mul | solution.py:28
  325.7 7.9 %mul.638 = f32[32,8,4096]{2,1,0:T(8,128)} reshape(f32[32,8,64,64]{3,2,1,0:T(8,128)} %get-tuple-element.53) | data formatting | bytes 8388608 | tf_op jit(solution)/shard_map/mul | solution.py:29
  333.6 7.9 %mul.641 = f32[32,8,4096]{2,1,0:T(8,128)} reshape(f32[32,8,64,64]{3,2,1,0:T(8,128)} %get-tuple-element.54) | data formatting | bytes 8388608 | tf_op jit(solution)/shard_map/mul | solution.py:28
  341.5 7.9 %mul.642 = f32[32,8,4096]{2,1,0:T(8,128)} reshape(f32[32,8,64,64]{3,2,1,0:T(8,128)} %get-tuple-element.55) | data formatting | bytes 8388608 | tf_op jit(solution)/shard_map/mul | solution.py:29
  349.4 7.9 %mul.645 = f32[32,8,4096]{2,1,0:T(8,128)} reshape(f32[32,8,64,64]{3,2,1,0:T(8,128)} %get-tuple-element.56) | data formatting | bytes 8388608 | tf_op jit(solution)/shard_map/mul | solution.py:28
  357.3 7.9 %mul.646 = f32[32,8,4096]{2,1,0:T(8,128)} reshape(f32[32,8,64,64]{3,2,1,0:T(8,128)} %get-tuple-element.57) | data formatting | bytes 8388608 | tf_op jit(solution)/shard_map/mul | solution.py:29
  365.2 7.9 %mul.649 = f32[32,8,4096]{2,1,0:T(8,128)} reshape(f32[32,8,64,64]{3,2,1,0:T(8,128)} %get-tuple-element.58) | data formatting | bytes 8388608 | tf_op jit(solution)/shard_map/mul | solution.py:28
  373.1 7.9 %mul.650 = f32[32,8,4096]{2,1,0:T(8,128)} reshape(f32[32,8,64,64]{3,2,1,0:T(8,128)} %get-tuple-element.60) | data formatting | bytes 8388608 | tf_op jit(solution)/shard_map/mul | solution.py:29
  382.2 16.0 %all_gather.26 = bf16[32,4,2048]{2,1,0:T(4,128)(2,1)S(1)} all-gather(bf16[32,4,512]{2,1,0:T(4,128)(2,1)S(1)} %add_convert_fusion.6), channel_id=1, replica_groups=mesh['req'=8,'mdl'=4] {'mdl'}, dimensions={2}, use_global_device_ids=true | all-gather | bytes 655360 | tf_op jit(solution)/shard_map/all_gather | solution.py:227
  400.7 5.6 %convolution_convert_fusion = bf16[128,2048]{1,0:T(8,128)(2,1)} fusion(bf16[1024,2048]{1,0:T(8,128)(2,1)} %param.41, bf16[128,2048]{1,0:T(8,128)(2,1)S(1)} %reshape.351, bf16[2048,1024]{1,0:T(8,128)(2,1)} %param.40), kind=kOutput, calls=%fused_computation.29 | convolution fusion | flops 1074397184 | bytes 9437184 | tf_op jit(solution)/shard_map/dot_general | solution.py:14
  406.3 22.3 %add_select_fusion = f32[32,8,4096]{2,1,0:T(8,128)} fusion(f32[32,8,4096]{2,1,0:T(8,128)} %mul.650, f32[32,8,4096]{2,1,0:T(8,128)} %mul.649, f32[32,8,4096]{2,1,0:T(8,128)} %mul.647, f32[32,8,4096]{2,1,0:T(8,128)} %mul.646, f32[32,8,4096]{2,1,0:T(8,128)} %mul.645, f32[32,8,4096]{2,1,0:T(8,128)} %mul.643, f32[32,8,4096]{2,1,0:T(8,128)} %mul.642, ...), kind=kLoop, calls=%fused_computation.17 | loop fusion | flops 16777216 | bytes 58720384 | tf_op jit(solution)/shard_map/jit(_where)/select_n | solution.py:32
  (178 shorter events, 106.2 us)
Async XLA Ops:
  7.2 234.8 %copy-start = (bf16[512,2048]{1,0:T(8,128)(2,1)S(1)}, bf16[512,2048]{1,0:T(8,128)(2,1)}, u32[]{:S(2)}) copy-start(bf16[512,2048]{1,0:T(8,128)(2,1)} %param.33) | copy-start | bytes 6291460
  7.2 147.5 %all-gather.2.cloned.1.call-start = ((), (), s32[]{:S(2)}) async-start(), calls=%async_computation.5 | async-start | bytes 1310720 | tf_op jit(solution)/shard_map/all_gather | solution.py:185
  10.3 79.1 %copy-start.20 = (s32[1024]{0:T(1024)}, s32[1024]{0:T(1024)S(1)}, u32[]{:S(2)}) copy-start(s32[1024]{0:T(1024)S(1)} %pad_clamp_fusion.1) | copy-start | bytes 12292
  12.3 77.0 %all-to-all-start.1 = ((bf16[8,4,512]{2,1,0:T(4,128)(2,1)}), bf16[8,4,512]{2,1,0:T(4,128)(2,1)S(1)}, u32[]{:S(2)}, u32[]{:S(2)}) async-start(bf16[8,4,512]{2,1,0:T(4,128)(2,1)} %reshape.354), calls=%async_computation.1 | async-start | bytes 65536 | tf_op jit(solution)/shard_map/all_to_all | solution.py:155
  25.9 63.5 %copy-start.11 = (f32[1,2048]{1,0:T(1,128)}, f32[1,2048]{1,0:T(1,128)S(1)}, u32[]{:S(2)}) copy-start(f32[1,2048]{1,0:T(1,128)S(1)} %get-tuple-element.70) | copy-start | bytes 24580
  25.9 63.5 %copy-start.12 = (f32[1,2048]{1,0:T(1,128)}, f32[1,2048]{1,0:T(1,128)S(1)}, u32[]{:S(2)}) copy-start(f32[1,2048]{1,0:T(1,128)S(1)} %get-tuple-element.71) | copy-start | bytes 24580
  78.9 10.5 %copy-start.10 = (f32[32,4]{1,0:T(8,128)}, f32[32,4]{1,0:T(8,128)S(1)}, u32[]{:S(2)}) copy-start(f32[32,4]{1,0:T(8,128)S(1)} %add_sqrt_fusion.3) | copy-start | bytes 1540
  80.4 13.8 %copy-start.21 = (s32[1024]{0:T(1024)}, s32[1024]{0:T(1024)S(1)}, u32[]{:S(2)}) copy-start(s32[1024]{0:T(1024)S(1)} %pad_clamp_fusion) | copy-start | bytes 12292
  89.4 67.7 %all-to-all-start = ((f32[8,4,8,4096]{3,2,1,0:T(8,128)}), f32[8,4,8,4096]{3,2,1,0:T(8,128)}, u32[]{:S(2)}, u32[]{:S(2)}) async-start(f32[8,4,8,4096]{3,2,1,0:T(8,128)} %bitcast.175), calls=%async_computation | async-start | bytes 8388608 | tf_op jit(solution)/shard_map/all_to_all | solution.py:154
  94.2 286.9 %reduce-scatter.3.cloned.1.call-start = ((), (), s32[]{:S(2)}) async-start(), calls=%async_computation.6 | async-start | bytes 1310720 | tf_op jit(solution)/shard_map/reduce_scatter | solution.py:223
  162.2 14.1 %copy-start.5 = (f32[32,8,64]{2,1,0:T(8,128)S(1)}, f32[32,8,64]{2,1,0:T(8,128)}, u32[]{:S(2)}) copy-start(f32[32,8,64]{2,1,0:T(8,128)} %copy.91) | copy-start | bytes 196612
  162.2 14.1 %copy-start.19 = (pred[32]{0:T(512)(128)(4,1)S(1)}, pred[32]{0:T(512)(128)(4,1)}, u32[]{:S(2)}) copy-start(pred[32]{0:T(512)(128)(4,1)} %get-tuple-element.83) | copy-start | bytes 100
  170.5 5.8 %copy-start.8 = (f32[32,8,64]{2,1,0:T(8,128)S(1)}, f32[32,8,64]{2,1,0:T(8,128)}, u32[]{:S(2)}) copy-start(f32[32,8,64]{2,1,0:T(8,128)} %get-tuple-element.35) | copy-start | bytes 196612
  170.5 18.2 %copy-start.22 = (pred[32]{0:T(512)(128)(4,1)S(1)}, pred[32]{0:T(512)(128)(4,1)}, u32[]{:S(2)}) copy-start(pred[32]{0:T(512)(128)(4,1)} %get-tuple-element.82) | copy-start | bytes 100
  188.7 19.5 %copy-start.4 = (f32[32,8,64]{2,1,0:T(8,128)S(1)}, f32[32,8,64]{2,1,0:T(8,128)}, u32[]{:S(2)}) copy-start(f32[32,8,64]{2,1,0:T(8,128)} %copy.96) | copy-start | bytes 196612
  188.7 19.5 %copy-start.18 = (pred[32]{0:T(512)(128)(4,1)S(1)}, pred[32]{0:T(512)(128)(4,1)}, u32[]{:S(2)}) copy-start(pred[32]{0:T(512)(128)(4,1)} %get-tuple-element.81) | copy-start | bytes 100
  208.3 13.9 %copy-start.7 = (f32[32,8,64]{2,1,0:T(8,128)S(1)}, f32[32,8,64]{2,1,0:T(8,128)}, u32[]{:S(2)}) copy-start(f32[32,8,64]{2,1,0:T(8,128)} %get-tuple-element.49) | copy-start | bytes 196612
  222.2 19.8 %copy-start.16 = (f32[1,512]{1,0:T(1,128)S(1)}, f32[1,512]{1,0:T(1,128)}, u32[]{:S(2)}) copy-start(f32[1,512]{1,0:T(1,128)} %get-tuple-element.73) | copy-start | bytes 6148
  222.2 19.8 %copy-start.17 = (f32[1,512]{1,0:T(1,128)S(1)}, f32[1,512]{1,0:T(1,128)}, u32[]{:S(2)}) copy-start(f32[1,512]{1,0:T(1,128)} %get-tuple-element.79) | copy-start | bytes 6148
  237.7 7.1 %copy-start.3 = (bf16[32,512]{1,0:T(8,128)(2,1)S(1)}, bf16[32,512]{1,0:T(8,128)(2,1)}, u32[]{:S(2)}) copy-start(bf16[32,512]{1,0:T(8,128)(2,1)} %param.26) | copy-start | bytes 98308
  237.7 13.0 %copy-start.26 = (s32[32]{0:T(128)S(1)}, s32[32]{0:T(128)}, u32[]{:S(2)}) copy-start(s32[32]{0:T(128)} %param.22) | copy-start | bytes 388
  237.7 13.1 %copy-start.24 = (pred[32,4]{0,1:T(4,128)(4,1)S(1)}, pred[32,4]{0,1:T(4,128)(4,1)}, u32[]{:S(2)}) copy-start(pred[32,4]{0,1:T(4,128)(4,1)} %get-tuple-element.84) | copy-start | bytes 388
  246.2 9.4 %all-to-all-start.2 = ((bf16[8,4,512]{2,1,0:T(4,128)(2,1)}), bf16[8,4,512]{2,1,0:T(4,128)(2,1)S(1)}, u32[]{:S(2)}, u32[]{:S(2)}) async-start(bf16[8,4,512]{2,1,0:T(4,128)(2,1)} %reshape.356), calls=%async_computation.3 | async-start | bytes 65536 | tf_op jit(solution)/shard_map/all_to_all | solution.py:156
  250.7 179.8 %reduce-scatter.5.cloned.1.call-start = ((), (), s32[]{:S(2)}) async-start(), calls=%async_computation.7 | async-start | bytes 655360 | tf_op jit(solution)/shard_map/reduce_scatter | solution.py:239
  274.9 8.1 %copy-start.6 = (f32[32,8,64]{2,1,0:T(8,128)S(1)}, f32[32,8,64]{2,1,0:T(8,128)}, u32[]{:S(2)}) copy-start(f32[32,8,64]{2,1,0:T(8,128)} %get-tuple-element.50) | copy-start | bytes 196612
  373.1 9.0 %copy-start.9 = (bf16[32,4,512]{2,1,0:T(4,128)(2,1)S(1)}, bf16[32,4,512]{2,1,0:T(4,128)(2,1)}, u32[]{:S(2)}) copy-start(bf16[32,4,512]{2,1,0:T(4,128)(2,1)} %param.21) | copy-start | bytes 393220
  373.1 25.9 %copy-start.13 = (f32[1,2048]{1,0:T(1,128)S(1)}, f32[1,2048]{1,0:T(1,128)}, u32[]{:S(2)}) copy-start(f32[1,2048]{1,0:T(1,128)} %get-tuple-element.69) | copy-start | bytes 24580
  373.1 25.9 %copy-start.14 = (f32[1,2048]{1,0:T(1,128)S(1)}, f32[1,2048]{1,0:T(1,128)}, u32[]{:S(2)}) copy-start(f32[1,2048]{1,0:T(1,128)} %get-tuple-element.72) | copy-start | bytes 24580
  373.1 26.3 %copy-start.15 = (f32[1,2048]{1,0:T(1,128)S(1)}, f32[1,2048]{1,0:T(1,128)}, u32[]{:S(2)}) copy-start(f32[1,2048]{1,0:T(1,128)} %get-tuple-element.62) | copy-start | bytes 24580
  382.2 24.1 %copy-start.23 = (pred[32]{0:T(512)(128)(4,1)S(1)}, pred[32]{0:T(512)(128)(4,1)}, u32[]{:S(2)}) copy-start(pred[32]{0:T(512)(128)(4,1)} %get-tuple-element.82) | copy-start | bytes 100
  382.2 24.1 %copy-start.25 = (pred[32]{0:T(512)(128)(4,1)S(1)}, pred[32]{0:T(512)(128)(4,1)}, u32[]{:S(2)}) copy-start(pred[32]{0:T(512)(128)(4,1)} %get-tuple-element.80) | copy-start | bytes 100
  406.3 26.0 %copy-start.1 = (bf16[512,2048]{1,0:T(8,128)(2,1)S(1)}, bf16[512,2048]{1,0:T(8,128)(2,1)}, u32[]{:S(2)}) copy-start(bf16[512,2048]{1,0:T(8,128)(2,1)} %param.33) | copy-start | bytes 6291460
  (1 other events, 5.8 us)
Sparse Core Ops, SparseCore 0:
  9.6 36.9 all-gather.1
  244.9 30.9 reduce-scatter.2
  406.4 20.1 reduce-scatter.4
where the time goes:
time: 445 us; the launch traced here: 439 us
  local copies, waits for them, and re-layouts  175 us (39%)
  other arithmetic  112 us (25%)
  blocking collectives  94.6 us (21%)
  matrix products  23 us (5%)
  starting transfers between devices  14.6 us (3%)
  between operations  14.5 us (3%)
  waiting for transfers between devices  5.32 us (1%)
    mul x9, local copies, waits for them, and re-layouts, advance(): wkv_square * decay_now[:, :, None, :]  48.5 us
    mul x10, local copies, waits for them, and re-layouts, advance(): value_now[..., None] * key_now[:, :, None, :]  37.6 us
    mul x4, local copies, waits for them, and re-layouts, advance(): removal[..., None] * (unit_now * alpha_now)[:, :, None, :]  31.6 us
    reduce_sum x2, other arithmetic, advance(): removal = -jnp.sum(wkv_square * unit_now[:, :, None, :], axis=-1)  24.5 us
    reduce_sum x2, other arithmetic, advance(): jnp.sum(updated * recept_now[:, :, None, :], axis=-1)  23.4 us
    dot_general x8, matrix products, project(): return jnp.dot(inputs, weight, preferred_element_type=jnp.float32)  23 us
    select_n x1, other arithmetic, advance(): jnp.where(is_valid[:, None, None, None], updated, wkv_square)  22.3 us
    all_gather x1, blocking collectives, per_device(): lax.all_gather(decay_down, 'mdl', axis=0, tiled=True)  20.2 us
  transfers between devices with their start and end apart: 6, of which 1 were waited for; matrix products, arithmetic and copies ran while one was open for 48% of the time, Pallas kernels for 0%

commit v1 on v0

--- a/solution.py
+++ b/solution.py
@@ -2,6 +2,35 @@
 import jax.numpy as jnp
 from jax import lax
 from jax.sharding import PartitionSpec as P
+
+
+def deliver_the_links(local_values, join_dim, buf):
+    seen_now, s_next = (local_values.shape[:join_dim], local_values.shape[join_dim + 1 :])
+    field_out = local_values.reshape(*seen_now, buf, -1, *s_next)
+    return jnp.moveaxis(field_out, join_dim, 0)
+
+
+def do_shapes(inner_x, out_dim):
+    inner_x = jnp.moveaxis(inner_x, 0, out_dim)
+    carry_out = inner_x.shape
+    return inner_x.reshape(
+        *carry_out[:out_dim], carry_out[out_dim] * carry_out[out_dim + 1], *carry_out[out_dim + 2 :]
+    )
+
+
+def take_halves(field_in, dev_axis, matrix, message):
+    x_next = lax.axis_size(dev_axis)
+    r_now = lax.axis_index(dev_axis)
+    a_next, now = (x_next, r_now)
+    part_next = deliver_the_links(field_in, matrix, a_next)
+    windows = [part_next[now]]
+    for ii in tuple(range(1, a_next)):
+        piece_now = part_next[now ^ ii]
+        res = lax.ppermute(piece_now, axis_name=dev_axis, perm=[(d, d ^ ii) for d in range(a_next)])
+        windows.append(res)
+    top = jnp.stack(windows)
+    part_next = top[now ^ jnp.arange(a_next)]
+    return do_shapes(part_next, message)
 
 
 def layer_norm(stream, gain_row, offset):
@@ -153,7 +182,7 @@
     got_state, got_att, got_ffn = (
         lax.all_to_all(sent_state, "req", split_axis=0, concat_axis=0, tiled=True),
         lax.all_to_all(sent_att, "req", split_axis=0, concat_axis=0, tiled=True),
-        lax.all_to_all(sent_ffn, "req", split_axis=0, concat_axis=0, tiled=True),
+        take_halves(sent_ffn, "req", matrix=0, message=0),
     )
     moved_state = got_state.reshape((sequence_batch_count,) + wkv_state.shape[1:])[placing]
     moved_att = got_att.reshape(sequence_batch_count, local_width)[placing].astype(jnp.bfloat16)

time: 445 us -> 451 us (1.013)
  local copies, waits for them, and re-layouts: 175 us -> 180 us
    ppermute x0 -> x7, starting transfers between devices: none -> 7.73 us  [take_halves(): lax.ppermute(piece_now, axis_name=dev_axis, perm=[(d, d ^ ii) for d in ra...]
    all_to_all x1 -> x0, waiting for transfers between devices: 4.6 us -> none  [per_device(): lax.all_to_all(sent_ffn, 'req', split_axis=0, concat_axis=0, tiled=True)]
    all_to_all x1 -> x0, starting transfers between devices: 4.53 us -> none  [per_device(): lax.all_to_all(sent_ffn, 'req', split_axis=0, concat_axis=0, tiled=True)]
  transfers between devices with their start and end apart: 6 -> 12, of which waited for: 1 -> 2; matrix products, arithmetic and copies ran while one was open for 48% -> 69% of each run, Pallas kernels for 0% -> 0%
where the time goes in v1:
time: 451 us; the launch traced here: 445 us
  local copies, waits for them, and re-layouts  180 us (40%)
  other arithmetic  113 us (25%)
  blocking collectives  92.7 us (21%)
  matrix products  23 us (5%)
  starting transfers between devices  16.3 us (4%)
  between operations  14.6 us (3%)
  waiting for transfers between devices  4.84 us (1%)
    mul x9, local copies, waits for them, and re-layouts, advance(): wkv_square * decay_now[:, :, None, :]  48.5 us
    mul x10, local copies, waits for them, and re-layouts, advance(): value_now[..., None] * key_now[:, :, None, :]  37.6 us
    mul x4, local copies, waits for them, and re-layouts, advance(): removal[..., None] * (unit_now * alpha_now)[:, :, None, :]  31.6 us
    reduce_sum x2, other arithmetic, advance(): removal = -jnp.sum(wkv_square * unit_now[:, :, None, :], axis=-1)  24.5 us
    reduce_sum x2, other arithmetic, advance(): jnp.sum(updated * recept_now[:, :, None, :], axis=-1)  23.4 us
    dot_general x8, matrix products, project(): return jnp.dot(inputs, weight, preferred_element_type=jnp.float32)  23 us
    select_n x1, other arithmetic, advance(): jnp.where(is_valid[:, None, None, None], updated, wkv_square)  22.3 us
    all_gather x1, blocking collectives, per_device(): lax.all_gather(decay_down, 'mdl', axis=0, tiled=True)  17.5 us
  transfers between devices with their start and end apart: 12, of which 2 were waited for; matrix products, arithmetic and copies ran while one was open for 69% of the time, Pallas kernels for 0%

profile of v1, /device:TPU:0, one launch (start us, length us, event | category | flops | bytes accessed | tf_op | source)
XLA Modules:
  0.0 444.6 jit_solution(396285596970733807)
XLA Ops:
  20.3 3.9 all-to-all-start.1
  35.6 17.5 %all_gather.23 = bf16[2048,96]{0,1:T(8,128)(2,1)} all-gather(bf16[512,96]{0,1:T(8,128)(2,1)} %param.34), channel_id=1, replica_groups=mesh['req'=8,'mdl'=4] {'mdl'}, dimensions={0}, use_global_device_ids=true | all-gather | bytes 491520 | tf_op jit(solution)/shard_map/all_gather | solution.py:212
  53.1 15.3 %all_gather.24 = bf16[2048,96]{0,1:T(8,128)(2,1)S(1)} all-gather(bf16[512,96]{0,1:T(8,128)(2,1)} %param.36), channel_id=1, replica_groups=mesh['req'=8,'mdl'=4] {'mdl'}, dimensions={0}, use_global_device_ids=true | all-gather | bytes 491520 | tf_op jit(solution)/shard_map/all_gather | solution.py:213
  68.5 15.5 %all_gather.21 = bf16[32,4,2048]{2,1,0:T(4,128)(2,1)S(1)} all-gather(bf16[32,4,512]{2,1,0:T(4,128)(2,1)} %param.21), channel_id=1, replica_groups=mesh['req'=8,'mdl'=4] {'mdl'}, dimensions={2}, use_global_device_ids=true | all-gather | bytes 655360 | tf_op jit(solution)/shard_map/all_gather | solution.py:190
  86.8 3.9 copy.89
  90.7 5.0 %gather_fusion = f32[32,8,4096]{2,1,0:T(8,128)} fusion(f32[32,8,4096]{2,1,0:T(8,128)} %param.24, s32[1024]{0:T(1024)S(1)} %pad_clamp_fusion.2), kind=kCustom, calls=%fused_computation | custom fusion | bytes 8388736 | tf_op jit(solution)/shard_map/gather | solution.py:179
  95.7 4.6 %all-to-all-start = ((f32[8,4,8,4096]{3,2,1,0:T(8,128)}), f32[8,4,8,4096]{3,2,1,0:T(8,128)}, u32[]{:S(2)}, u32[]{:S(2)}) async-start(f32[8,4,8,4096]{3,2,1,0:T(8,128)} %bitcast.206), calls=%async_computation | async-start | bytes 8388608 | tf_op jit(solution)/shard_map/all_to_all | solution.py:183
  101.0 13.9 %all_gather.22 = bf16[32,2048]{1,0:T(8,128)(2,1)S(1)} all-gather(bf16[32,512]{1,0:T(8,128)(2,1)S(1)} %gather_fusion.3), channel_id=1, replica_groups=mesh['req'=8,'mdl'=4] {'mdl'}, dimensions={1}, use_global_device_ids=true | all-gather | bytes 163840 | tf_op jit(solution)/shard_map/all_gather | solution.py:194
  126.5 4.4 add_convert_fusion.5
  163.4 5.1 %gather_fusion.1 = f32[32,8,4096]{2,1,0:T(8,128)} fusion(f32[32,8,4096]{2,1,0:T(8,128)} %bitcast.1, s32[1024]{0:T(1024)} %copy-done.21), kind=kCustom, calls=%fused_computation.1 | custom fusion | bytes 8388736 | tf_op jit(solution)/shard_map/gather | solution.py:187
  168.6 8.0 %reshape.359 = f32[32,8,64,64]{3,2,1,0:T(8,128)} reshape(f32[32,8,4096]{2,1,0:T(8,128)} %gather_fusion.1) | data formatting | bytes 8388608 | tf_op jit(solution)/shard_map/reshape | solution.py:90
  176.6 5.8 %multiply_reduce_fusion.7 = f32[32,8,64]{2,1,0:T(8,128)S(1)} fusion(f32[32,8,64,64]{3,2,1,0:T(8,128)} %reshape.359, f32[32,8,64]{2,1,0:T(8,128)S(1)} %get-tuple-element.98), kind=kLoop, calls=%fused_computation.17 | loop fusion | flops 2080768 | bytes 4325376 | tf_op jit(solution)/shard_map/reduce_sum | solution.py:54
  182.4 11.0 %multiply_reduce_fusion.6 = (f32[32,8,64]{2,1,0:T(8,128)S(1)}, f32[32,8,64]{2,1,0:T(8,128)S(1)}) fusion(f32[32,8,64]{2,1,0:T(8,128)S(1)} %copy-done.7, f32[32,8,64,64]{3,2,1,0:T(8,128)S(1)} %copy-done.2, f32[32,8,64]{2,1,0:T(8,128)S(1)} %get-tuple-element.51, f32[32,8,64]{2,1,0:T(8,128)S(1)} %get-tuple-element.30, f32[32,8,64]{2,1,0:T(8,128)S(1)} %neg.38, ...), kind=kLoop, calls=%fused_computation.15 | loop fusion | flops 10452992 | bytes 4784160 | tf_op jit(solution)/shard_map/reduce_sum | solution.py:60
  194.8 18.7 %multiply_reduce_fusion.3 = (f32[32,8,64]{2,1,0:T(8,128)S(1)}, f32[32,8,64,64]{3,2,1,0:T(8,128)}, f32[32,8,64]{2,1,0:T(8,128)S(1)}, f32[32,8,64,64]{3,2,1,0:T(8,...) fusion(f32[32,8,64]{2,1,0:T(8,128)} %get-tuple-element.100, ...), kind=kLoop, calls=%fused_computation.11 | loop fusion | flops 16744448 | bytes 26083392 | tf_op jit(solution)/shard_map/reduce_sum | solution.py:54
  214.3 12.5 %multiply_reduce_fusion.2 = (f32[32,8,64]{2,1,0:T(8,128)S(1)}, f32[32,8,64]{2,1,0:T(8,128)S(1)}, f32[32,8,64,64]{3,2,1,0:T(8,128)}, f32[32,8,64,64]{3,2,1,0:T(8,128)}) fusion(f32[32,8,64]{2,1,0:T(8,128)} %get-tuple-element.34, f32[32,8,64,64]{3,2,1,0:T(8,128)} %get-tuple-element.18, f32[32,8,64]{2,1,0:T(8,128)S(1)} %get-tuple-element.48, ...), kind=kLoop, calls=%fused_computation.9 | loop fusion | flops 10452992 | bytes 13172768 | tf_op jit(solution)/shard_map/reduce_sum | solution.py:60
  228.2 15.5 %broadcast_multiply_fusion.1 = (f32[32,8,64,64]{3,2,1,0:T(8,128)}, f32[32,8,64]{2,1,0:T(8,128)S(1)}, f32[32,8,64,64]{3,2,1,0:T(8,128)}) fusion(f32[32,8,64]{2,1,0:T(8,128)} %get-tuple-element.31, f32[32,8,64]{2,1,0:T(8,128)} %neg.42, f32[32,8,64]{2,1,0:T(8,128)} %get-tuple-element.33, f32[32,8,64]{2,1,0:T(8,128)} %get-tuple-element.40, ...), kind=kLoop, calls=%fused_computation.20 | loop fusion | flops 13615104 | bytes 13369376 | tf_op jit(solution)/shard_map/mul | solution.py:57
  261.9 14.6 %all_gather.27 = bf16[32,2048]{1,0:T(8,128)(2,1)S(1)} all-gather(bf16[32,512]{1,0:T(8,128)(2,1)S(1)} %gather_fusion.6), channel_id=1, replica_groups=mesh['req'=8,'mdl'=4] {'mdl'}, dimensions={1}, use_global_device_ids=true | all-gather | bytes 163840 | tf_op jit(solution)/shard_map/all_gather | solution.py:195
  280.5 8.1 %mul.647 = f32[32,8,4096]{2,1,0:T(8,128)} reshape(f32[32,8,64,64]{3,2,1,0:T(8,128)} %mul.597) | data formatting | bytes 8388608 | tf_op jit(solution)/shard_map/mul | solution.py:56
  292.4 7.9 %mul.639 = f32[32,8,4096]{2,1,0:T(8,128)} reshape(f32[32,8,64,64]{3,2,1,0:T(8,128)} %mul.561) | data formatting | bytes 8388608 | tf_op jit(solution)/shard_map/mul | solution.py:56
  304.0 7.9 %mul.643 = f32[32,8,4096]{2,1,0:T(8,128)} reshape(f32[32,8,64,64]{3,2,1,0:T(8,128)} %mul.579) | data formatting | bytes 8388608 | tf_op jit(solution)/shard_map/mul | solution.py:56
  315.6 7.9 %mul.635 = f32[32,8,4096]{2,1,0:T(8,128)} reshape(f32[32,8,64,64]{3,2,1,0:T(8,128)} %mul.523) | data formatting | bytes 8388608 | tf_op jit(solution)/shard_map/mul | solution.py:56
  323.5 7.9 %mul.637 = f32[32,8,4096]{2,1,0:T(8,128)} reshape(f32[32,8,64,64]{3,2,1,0:T(8,128)} %get-tuple-element.52) | data formatting | bytes 8388608 | tf_op jit(solution)/shard_map/mul | solution.py:57
  331.4 7.9 %mul.638 = f32[32,8,4096]{2,1,0:T(8,128)} reshape(f32[32,8,64,64]{3,2,1,0:T(8,128)} %get-tuple-element.53) | data formatting | bytes 8388608 | tf_op jit(solution)/shard_map/mul | solution.py:58
  339.3 7.9 %mul.641 = f32[32,8,4096]{2,1,0:T(8,128)} reshape(f32[32,8,64,64]{3,2,1,0:T(8,128)} %get-tuple-element.54) | data formatting | bytes 8388608 | tf_op jit(solution)/shard_map/mul | solution.py:57
  347.2 7.9 %mul.642 = f32[32,8,4096]{2,1,0:T(8,128)} reshape(f32[32,8,64,64]{3,2,1,0:T(8,128)} %get-tuple-element.55) | data formatting | bytes 8388608 | tf_op jit(solution)/shard_map/mul | solution.py:58
  355.1 7.9 %mul.645 = f32[32,8,4096]{2,1,0:T(8,128)} reshape(f32[32,8,64,64]{3,2,1,0:T(8,128)} %get-tuple-element.56) | data formatting | bytes 8388608 | tf_op jit(solution)/shard_map/mul | solution.py:57
  363.0 7.9 %mul.646 = f32[32,8,4096]{2,1,0:T(8,128)} reshape(f32[32,8,64,64]{3,2,1,0:T(8,128)} %get-tuple-element.57) | data formatting | bytes 8388608 | tf_op jit(solution)/shard_map/mul | solution.py:58
  370.9 7.9 %mul.649 = f32[32,8,4096]{2,1,0:T(8,128)} reshape(f32[32,8,64,64]{3,2,1,0:T(8,128)} %get-tuple-element.58) | data formatting | bytes 8388608 | tf_op jit(solution)/shard_map/mul | solution.py:57
  378.8 7.9 %mul.650 = f32[32,8,4096]{2,1,0:T(8,128)} reshape(f32[32,8,64,64]{3,2,1,0:T(8,128)} %get-tuple-element.60) | data formatting | bytes 8388608 | tf_op jit(solution)/shard_map/mul | solution.py:58
  387.9 15.9 %all_gather.26 = bf16[32,4,2048]{2,1,0:T(4,128)(2,1)S(1)} all-gather(bf16[32,4,512]{2,1,0:T(4,128)(2,1)S(1)} %add_convert_fusion.6), channel_id=1, replica_groups=mesh['req'=8,'mdl'=4] {'mdl'}, dimensions={2}, use_global_device_ids=true | all-gather | bytes 655360 | tf_op jit(solution)/shard_map/all_gather | solution.py:256
  406.2 5.6 %convolution_convert_fusion = bf16[128,2048]{1,0:T(8,128)(2,1)} fusion(bf16[1024,2048]{1,0:T(8,128)(2,1)} %param.41, bf16[128,2048]{1,0:T(8,128)(2,1)S(1)} %reshape.371, bf16[2048,1024]{1,0:T(8,128)(2,1)} %param.40), kind=kOutput, calls=%fused_computation.30 | convolution fusion | flops 1074397184 | bytes 9437184 | tf_op jit(solution)/shard_map/dot_general | solution.py:43
  411.8 22.3 %add_select_fusion = f32[32,8,4096]{2,1,0:T(8,128)} fusion(f32[32,8,4096]{2,1,0:T(8,128)} %mul.650, f32[32,8,4096]{2,1,0:T(8,128)} %mul.649, f32[32,8,4096]{2,1,0:T(8,128)} %mul.647, f32[32,8,4096]{2,1,0:T(8,128)} %mul.646, f32[32,8,4096]{2,1,0:T(8,128)} %mul.645, f32[32,8,4096]{2,1,0:T(8,128)} %mul.643, f32[32,8,4096]{2,1,0:T(8,128)} %mul.642, ...), kind=kLoop, calls=%fused_computation.18 | loop fusion | flops 16777216 | bytes 58720384 | tf_op jit(solution)/shard_map/jit(_where)/select_n | solution.py:61
  (205 shorter events, 116.1 us)
Async XLA Ops:
  7.2 240.9 %copy-start = (bf16[512,2048]{1,0:T(8,128)(2,1)S(1)}, bf16[512,2048]{1,0:T(8,128)(2,1)}, u32[]{:S(2)}) copy-start(bf16[512,2048]{1,0:T(8,128)(2,1)} %param.33) | copy-start | bytes 6291460
  7.2 153.9 %all-gather.2.cloned.1.call-start = ((), (), s32[]{:S(2)}) async-start(), calls=%async_computation.4 | async-start | bytes 1310720 | tf_op jit(solution)/shard_map/all_gather | solution.py:214
  12.4 247.4 %collective-permute-start.6 = (bf16[1,4,512]{2,1,0:T(4,128)(2,1)}, bf16[1,4,512]{2,1,0:T(4,128)(2,1)}, u32[]{:S(2)}, u32[]{:S(2)}) collective-permute-start(bf16[1,4,512]{2,1,0:T(4,128)(2,1)} %get-tuple-element.69), channel_id=1, source_target_pairs={{0,28},{4,24},{8,20},{12,16},{16,12},{20,8},{24,4},{28,0},{1,29},{... | collective-permute-start | bytes 12296 | tf_op jit(solution)/shard_map/ppermute | solution.py:29
  15.8 243.4 %collective-permute-start.5 = (bf16[1,4,512]{2,1,0:T(4,128)(2,1)}, bf16[1,4,512]{2,1,0:T(4,128)(2,1)}, u32[]{:S(2)}, u32[]{:S(2)}) collective-permute-start(bf16[1,4,512]{2,1,0:T(4,128)(2,1)} %get-tuple-element.70), channel_id=1, source_target_pairs={{0,24},{4,28},{8,16},{12,20},{16,8},{20,12},{24,0},{28,4},{1,25},{... | collective-permute-start | bytes 12296 | tf_op jit(solution)/shard_map/ppermute | solution.py:29
  16.4 242.0 %collective-permute-start.4 = (bf16[1,4,512]{2,1,0:T(4,128)(2,1)}, bf16[1,4,512]{2,1,0:T(4,128)(2,1)}, u32[]{:S(2)}, u32[]{:S(2)}) collective-permute-start(bf16[1,4,512]{2,1,0:T(4,128)(2,1)} %get-tuple-element.71), channel_id=1, source_target_pairs={{0,20},{4,16},{8,28},{12,24},{16,4},{20,0},{24,12},{28,8},{1,21},{... | collective-permute-start | bytes 12296 | tf_op jit(solution)/shard_map/ppermute | solution.py:29
  17.8 239.9 %collective-permute-start.3 = (bf16[1,4,512]{2,1,0:T(4,128)(2,1)}, bf16[1,4,512]{2,1,0:T(4,128)(2,1)}, u32[]{:S(2)}, u32[]{:S(2)}) collective-permute-start(bf16[1,4,512]{2,1,0:T(4,128)(2,1)} %get-tuple-element.72), channel_id=1, source_target_pairs={{0,16},{4,20},{8,24},{12,28},{16,0},{20,4},{24,8},{28,12},{1,17},{... | collective-permute-start | bytes 12296 | tf_op jit(solution)/shard_map/ppermute | solution.py:29
  18.1 232.9 %collective-permute-start = (bf16[1,4,512]{2,1,0:T(4,128)(2,1)}, bf16[1,4,512]{2,1,0:T(4,128)(2,1)}, u32[]{:S(2)}, u32[]{:S(2)}) collective-permute-start(bf16[1,4,512]{2,1,0:T(4,128)(2,1)} %get-tuple-element.75), channel_id=1, source_target_pairs={{0,4},{4,0},{8,12},{12,8},{16,20},{20,16},{24,28},{28,24},{1,5},{5... | collective-permute-start | bytes 12296 | tf_op jit(solution)/shard_map/ppermute | solution.py:29
  20.3 75.4 %all-to-all-start.1 = ((bf16[8,4,512]{2,1,0:T(4,128)(2,1)}), bf16[8,4,512]{2,1,0:T(4,128)(2,1)S(1)}, u32[]{:S(2)}, u32[]{:S(2)}) async-start(bf16[8,4,512]{2,1,0:T(4,128)(2,1)} %reshape.374), calls=%async_computation.1 | async-start | bytes 65536 | tf_op jit(solution)/shard_map/all_to_all | solution.py:184
  32.3 68.1 %copy-start.21 = (s32[1024]{0:T(1024)}, s32[1024]{0:T(1024)S(1)}, u32[]{:S(2)}) copy-start(s32[1024]{0:T(1024)S(1)} %pad_clamp_fusion.1) | copy-start | bytes 12292
  33.8 61.9 %copy-start.10 = (f32[1,2048]{1,0:T(1,128)}, f32[1,2048]{1,0:T(1,128)S(1)}, u32[]{:S(2)}) copy-start(f32[1,2048]{1,0:T(1,128)S(1)} %get-tuple-element.78) | copy-start | bytes 24580
  33.8 61.9 %copy-start.11 = (f32[1,2048]{1,0:T(1,128)}, f32[1,2048]{1,0:T(1,128)S(1)}, u32[]{:S(2)}) copy-start(f32[1,2048]{1,0:T(1,128)S(1)} %get-tuple-element.79) | copy-start | bytes 24580
  84.8 11.0 %copy-start.9 = (f32[32,4]{1,0:T(8,128)}, f32[32,4]{1,0:T(8,128)S(1)}, u32[]{:S(2)}) copy-start(f32[32,4]{1,0:T(8,128)S(1)} %add_sqrt_fusion.3) | copy-start | bytes 1540
  95.7 67.7 %all-to-all-start = ((f32[8,4,8,4096]{3,2,1,0:T(8,128)}), f32[8,4,8,4096]{3,2,1,0:T(8,128)}, u32[]{:S(2)}, u32[]{:S(2)}) async-start(f32[8,4,8,4096]{3,2,1,0:T(8,128)} %bitcast.206), calls=%async_computation | async-start | bytes 8388608 | tf_op jit(solution)/shard_map/all_to_all | solution.py:183
  100.3 286.4 %reduce-scatter.3.cloned.1.call-start = ((), (), s32[]{:S(2)}) async-start(), calls=%async_computation.5 | async-start | bytes 1310720 | tf_op jit(solution)/shard_map/reduce_scatter | solution.py:252
  168.6 13.8 %copy-start.4 = (f32[32,8,64]{2,1,0:T(8,128)S(1)}, f32[32,8,64]{2,1,0:T(8,128)}, u32[]{:S(2)}) copy-start(f32[32,8,64]{2,1,0:T(8,128)} %copy.91) | copy-start | bytes 196612
  168.6 13.8 %copy-start.20 = (pred[32]{0:T(512)(128)(4,1)S(1)}, pred[32]{0:T(512)(128)(4,1)}, u32[]{:S(2)}) copy-start(pred[32]{0:T(512)(128)(4,1)} %get-tuple-element.91) | copy-start | bytes 100
  176.6 18.2 %copy-start.22 = (pred[32]{0:T(512)(128)(4,1)S(1)}, pred[32]{0:T(512)(128)(4,1)}, u32[]{:S(2)}) copy-start(pred[32]{0:T(512)(128)(4,1)} %get-tuple-element.90) | copy-start | bytes 100
  194.8 19.5 %copy-start.3 = (f32[32,8,64]{2,1,0:T(8,128)S(1)}, f32[32,8,64]{2,1,0:T(8,128)}, u32[]{:S(2)}) copy-start(f32[32,8,64]{2,1,0:T(8,128)} %copy.96) | copy-start | bytes 196612
  194.8 19.5 %copy-start.19 = (pred[32]{0:T(512)(128)(4,1)S(1)}, pred[32]{0:T(512)(128)(4,1)}, u32[]{:S(2)}) copy-start(pred[32]{0:T(512)(128)(4,1)} %get-tuple-element.89) | copy-start | bytes 100
  214.3 13.9 %copy-start.6 = (f32[32,8,64]{2,1,0:T(8,128)S(1)}, f32[32,8,64]{2,1,0:T(8,128)}, u32[]{:S(2)}) copy-start(f32[32,8,64]{2,1,0:T(8,128)} %get-tuple-element.49) | copy-start | bytes 196612
  228.2 19.9 %copy-start.17 = (f32[1,512]{1,0:T(1,128)S(1)}, f32[1,512]{1,0:T(1,128)}, u32[]{:S(2)}) copy-start(f32[1,512]{1,0:T(1,128)} %get-tuple-element.81) | copy-start | bytes 6148
  228.2 19.9 %copy-start.18 = (f32[1,512]{1,0:T(1,128)S(1)}, f32[1,512]{1,0:T(1,128)}, u32[]{:S(2)}) copy-start(f32[1,512]{1,0:T(1,128)} %get-tuple-element.87) | copy-start | bytes 6148
  250.8 185.3 %reduce-scatter.5.cloned.1.call-start = ((), (), s32[]{:S(2)}) async-start(), calls=%async_computation.6 | async-start | bytes 655360 | tf_op jit(solution)/shard_map/reduce_scatter | solution.py:268
  251.0 3.7 collective-permute-start.1
  254.7 3.0 collective-permute-start.2
  378.8 25.7 %copy-start.12 = (f32[1,2048]{1,0:T(1,128)S(1)}, f32[1,2048]{1,0:T(1,128)}, u32[]{:S(2)}) copy-start(f32[1,2048]{1,0:T(1,128)} %get-tuple-element.77) | copy-start | bytes 24580
  378.8 25.7 %copy-start.13 = (f32[1,2048]{1,0:T(1,128)S(1)}, f32[1,2048]{1,0:T(1,128)}, u32[]{:S(2)}) copy-start(f32[1,2048]{1,0:T(1,128)} %get-tuple-element.80) | copy-start | bytes 24580
  378.8 26.2 %copy-start.16 = (f32[1,2048]{1,0:T(1,128)S(1)}, f32[1,2048]{1,0:T(1,128)}, u32[]{:S(2)}) copy-start(f32[1,2048]{1,0:T(1,128)} %get-tuple-element.62) | copy-start | bytes 24580
  387.8 23.9 %copy-start.23 = (pred[32]{0:T(512)(128)(4,1)S(1)}, pred[32]{0:T(512)(128)(4,1)}, u32[]{:S(2)}) copy-start(pred[32]{0:T(512)(128)(4,1)} %get-tuple-element.90) | copy-start | bytes 100
  387.9 23.9 %copy-start.27 = (pred[32]{0:T(512)(128)(4,1)S(1)}, pred[32]{0:T(512)(128)(4,1)}, u32[]{:S(2)}) copy-start(pred[32]{0:T(512)(128)(4,1)} %get-tuple-element.88) | copy-start | bytes 100
  411.8 22.3 %copy-start.14 = (f32[32,4]{1,0:T(8,128)S(1)}, f32[32,4]{1,0:T(8,128)}, u32[]{:S(2)}) copy-start(f32[32,4]{1,0:T(8,128)} %fusion.54) | copy-start | bytes 1540
  411.8 26.0 %copy-start.1 = (bf16[512,2048]{1,0:T(8,128)(2,1)S(1)}, bf16[512,2048]{1,0:T(8,128)(2,1)}, u32[]{:S(2)}) copy-start(bf16[512,2048]{1,0:T(8,128)(2,1)} %param.33) | copy-start | bytes 6291460
  (9 other events, 70.5 us)
Sparse Core Ops, SparseCore 0:
  9.6 30.6 all-gather.1
  250.9 30.2 reduce-scatter.2
  411.9 22.5 reduce-scatter.4
